TPU v7x, 512 devices: a whole 4x8x8 slice. The times are simulated.
512 devices in a mesh: head: 8 (over y_hi, x), blk: 64 (over y_lo, z, core).
Axes of the slice: x: 4, y: 8 (y_hi: 2, y_lo: 4; y = y_hi * 4 + y_lo), z: 8, core: 2. Of those that a mesh axis runs over, the one named last changes fastest.
Arguments:
- query_rows: bfloat16 [8192, 1536], P(('head', 'blk')), may hold values from -400 to 400
- key_rows: bfloat16 [8192, 1536], P(('head', 'blk')), may hold values from -400 to 400
- value_rows: bfloat16 [8192, 1536], P(('head', 'blk')), may hold values from -6 to 6
- residual: bfloat16 [8192, 1536], P(('head', 'blk')), may hold values from -6 to 6
- out_weight: bfloat16 [1536, 1536], P('head'), may hold values from -0.15625 to 0.15625
- attention_gate: float32 [1536], replicated, may hold values from 0.5 to 1.5
- norm_shift: float32 [1536], replicated, may hold values from -1 to 1
- norm_scale: float32 [1536], replicated, may hold values from -0.5 to 0.5
- expert_gate: float32 [1536], replicated, may hold values from 0.5 to 1.5
- expert_up: bfloat16 [64, 1536, 4096], P('blk', None, 'head'), may hold values from -0.15625 to 0.15625
- expert_down: bfloat16 [64, 4096, 1536], P('blk', 'head'), may hold values from -0.09375 to 0.09375
- routing: int32 [8192, 2], P(('head', 'blk')), may hold values from 0 to 63, as said below
- combine_weight: float32 [8192, 2], P(('head', 'blk')), may hold values from 0.2 to 1
Outputs:
- mixed: bfloat16 [8192, 1536], P(('head', 'blk'))
Inputs may be any that keep to these rules, and one draw needn't show every extreme that they name: `routing`: the two choices of a token differ. Within the 16 tokens of one device every expert is named at most 2 times, and one expert, the same for every device, is named exactly 2 times by every device.
All inputs are finite; a program needn't handle non-finite values.
Results may differ from a plain program's by a relative error of at most 0.011.
Values may be sent and summed in bfloat16 or wider, within the bound.
No kernel may reach another device: no remote copies, remote signals or barrier semaphores. Data moves between devices by JAX's collectives and lax.ppermute only.
A program may use at most 64 MiB of HBM per device.

v0:
```python
import math

import jax
import jax.numpy as jnp
from jax import lax
from jax.sharding import Mesh
from jax.sharding import PartitionSpec as P

HD = 64
TOPK = 2
HEAD = ("head_0", "head_1")
HEAD_BLK = ("head_0", "head_1", "blk")


def sent_together(arrays, axis, dim, along):
    widths = [a.shape[along] for a in arrays]
    both = jnp.concatenate(arrays, axis=along)
    result = lax.all_gather(both, axis, axis=dim, tiled=True)
    return tuple(jnp.split(result, [sum(widths[:k]) for k in range(1, len(widths))], axis=along))


def cut_along(array, dim, devices):
    before, after = (array.shape[:dim], array.shape[dim + 1 :])
    return jnp.moveaxis(array.reshape(*before, devices, -1, *after), dim, 0)


def sum_at_owner(array, axis, dim):
    devices = lax.axis_size(axis)
    blocks = lax.all_to_all(cut_along(array, dim, devices), axis, 0, 0, tiled=True)
    return jnp.sum(blocks.astype(jnp.float32), axis=0)


def reduced_to_own(blocks, axes, order):
    shape = [lax.axis_size(a) for a in axes]
    blocks = blocks.reshape(*shape, *blocks.shape[1:])
    blocks = blocks.transpose(*order, *range(len(axes), blocks.ndim))
    blocks = blocks.reshape(-1, *blocks.shape[len(axes) :])
    for k in order:
        blocks = lax.psum_scatter(blocks, axes[k], scatter_dimension=0, tiled=True)
    return blocks[0]


def sum_by_axis_2(array, axes, order, dim):
    devices = lax.axis_size(axes)
    return reduced_to_own(cut_along(array, dim, devices), axes, order)


def on_device(
    query_rows,
    key_rows,
    value_rows,
    residual,
    out_weight,
    attention_gate,
    norm_shift,
    norm_scale,
    expert_gate,
    expert_up,
    expert_down,
    routing,
    combine_weight,
):
    tok_rows = query_rows.shape[0]
    model_width = query_rows.shape[1]
    block_count = lax.axis_size("blk")
    cap_slots = max(2, TOPK * tok_rows // block_count)
    query_heads, key_heads, value_heads = (
        lax.all_to_all(query_rows, HEAD, split_axis=1, concat_axis=0, tiled=True),
        lax.all_to_all(key_rows, HEAD, split_axis=1, concat_axis=0, tiled=True),
        lax.all_to_all(value_rows, HEAD, split_axis=1, concat_axis=0, tiled=True),
    )
    head_rows = query_heads.shape[0]
    head_cols = query_heads.shape[1]
    heads_here = head_cols // HD
    score_scale = 1.0 / math.sqrt(HD)
    query_split = query_heads.reshape(head_rows, heads_here, HD)
    peak_old = jnp.full((heads_here, head_rows), -1e30, jnp.float32)
    key_piece, value_piece = sent_together((key_heads, value_heads), "blk", 0, 1)
    piece_rows = key_piece.shape[0]
    key_split = key_piece.reshape(piece_rows, heads_here, HD)
    value_split = value_piece.reshape(piece_rows, heads_here, HD)
    scores = (
        jnp.einsum("rhd,phd->hrp", query_split, key_split, preferred_element_type=jnp.float32)
        * score_scale
    )
    peak_new = jnp.maximum(peak_old, jnp.max(scores, axis=2))
    weights = jnp.exp(scores - peak_new[:, :, None])
    total_new = jnp.sum(weights, axis=2)
    accum_new = jnp.einsum(
        "hrp,phd->hrd",
        weights.astype(jnp.bfloat16),
        value_split,
        preferred_element_type=jnp.float32,
    )
    attended = (
        jnp.transpose(accum_new / total_new[:, :, None], (1, 0, 2))
        .reshape(head_rows, head_cols)
        .astype(jnp.bfloat16)
    )
    projected = sum_at_owner(
        jnp.dot(attended, out_weight, preferred_element_type=jnp.float32).astype(jnp.bfloat16),
        HEAD,
        0,
    )
    middle = residual.astype(jnp.float32) + attention_gate * projected
    average = jnp.mean(middle, axis=1, keepdims=True)
    centered = middle - average
    variance = jnp.mean(centered * centered, axis=1, keepdims=True)
    normed = (centered * lax.rsqrt(variance + 1e-06) * (1.0 + norm_scale) + norm_shift).astype(
        jnp.bfloat16
    )
    flat_choice = routing.reshape(-1)
    onehot = (flat_choice[:, None] == jnp.arange(block_count, dtype=jnp.int32)[None, :]).astype(
        jnp.int32
    )
    earlier = jnp.cumsum(onehot, axis=0) - onehot
    slot_index = flat_choice * cap_slots + jnp.sum(earlier * onehot, axis=1)
    source_rows = jnp.repeat(normed, TOPK, axis=0)
    send_buffer = (
        jnp.zeros((block_count * cap_slots, model_width), jnp.bfloat16)
        .at[slot_index]
        .set(source_rows)
    )
    arrived = lax.all_to_all(send_buffer, "blk", split_axis=0, concat_axis=0, tiled=True)
    hidden = jax.nn.gelu(
        jnp.dot(
            lax.all_gather(arrived, HEAD, axis=0, tiled=True),
            expert_up[0],
            preferred_element_type=jnp.float32,
        ),
        approximate=True,
    ).astype(jnp.bfloat16)
    partial_sum = sum_by_axis_2(
        jnp.dot(hidden, expert_down[0], preferred_element_type=jnp.float32).astype(jnp.bfloat16),
        HEAD,
        (1, 0),
        0,
    ).astype(jnp.float32)
    returned_rows = lax.all_to_all(
        partial_sum.astype(jnp.bfloat16), "blk", split_axis=0, concat_axis=0, tiled=True
    )
    picked = returned_rows[slot_index].reshape(tok_rows, TOPK, model_width).astype(jnp.float32)
    mixture = jnp.sum(picked * combine_weight[:, :, None], axis=1)
    return (middle + expert_gate * mixture).astype(jnp.bfloat16)


def solution(mesh):
    split = Mesh(mesh.devices.reshape(2, 4, mesh.shape["blk"]), ("head_0", "head_1", "blk"))
    placed = (
        P(HEAD_BLK, None),
        P(HEAD_BLK, None),
        P(HEAD_BLK, None),
        P(HEAD_BLK, None),
        P(HEAD, None),
        P(),
        P(),
        P(),
        P(),
        P("blk", None, HEAD),
        P("blk", HEAD, None),
        P(HEAD_BLK, None),
        P(HEAD_BLK, None),
    )
    return jax.shard_map(
        on_device, mesh=split, in_specs=placed, out_specs=P(HEAD_BLK, None), check_vma=False
    )
```

profile of v0, /device:TPU:1, one launch (start us, length us, event | category | flops | bytes accessed | tf_op | source)
XLA Modules:
  0.0 451.4 jit_solution(9716654070342487757)
XLA Ops:
  6.5 1.0 all_to_all.63
  7.6 0.6 copy.22
  8.2 10.1 %all-to-all-start.1 = ((bf16[16,8,192]{2,0,1:T(8,128)(2,1)}), bf16[16,8,192]{2,0,1:T(8,128)(2,1)S(1)}, u32[]{:S(2)}, u32[]{:S(2)}) async-start(bf16[16,8,192]{2,0,1:T(8,128)(2,1)} %copy.22), calls=%async_computation.1 | async-start | bytes 131072 | tf_op jit(solution)/shard_map/all_to_all | solution.py:70
  18.3 0.0 all-gather.3.cloned.1.call-start
  18.3 0.9 all_to_all.59
  19.3 8.2 %all-to-all-done.1 = bf16[16,8,192]{2,0,1:T(8,128)(2,1)S(1)} async-done(((bf16[16,8,192]{2,0,1:T(8,128)(2,1)}), bf16[16,8,192]{2,0,1:T(8,128)(2,1)S(1)}, u32[]{:S(2)}, u32[]{:S(2)}) %all-to-all-start.1) | async-done | bytes 49184 | tf_op jit(solution)/shard_map/all_to_all | solution.py:70
  27.5 11.5 %all_to_all.83 = bf16[16,8,192]{2,0,1:T(8,128)(2,1)S(1)} all-to-all(bf16[16,8,192]{2,0,1:T(8,128)(2,1)S(1)} %copy.21), channel_id=1, replica_groups=mesh['head_0'=2,'head_1'=4,'blk'=64] {'head_0','head_1'}, dimensions={1} | all-to-all | bytes 98304 | tf_op jit(solution)/shard_map/all_to_all | solution.py:69
  39.0 0.7 pad_maximum_fusion
  39.7 0.0 all-gather.3.cloned.1.call-update
  39.7 0.9 all_to_all.67
  40.6 0.6 copy.24
  41.3 3.3 all-to-all-start.2
  44.6 0.7 broadcast_multiply_fusion
  45.3 0.8 copy.29
  46.1 0.1 copy.28
  46.2 0.1 mul.100
  46.3 0.1 eq.15
  46.3 7.3 %all-to-all-done.2 = bf16[16,8,192]{2,0,1:T(8,128)(2,1)S(1)} async-done(((bf16[16,8,192]{2,0,1:T(8,128)(2,1)}), bf16[16,8,192]{2,0,1:T(8,128)(2,1)S(1)}, u32[]{:S(2)}, u32[]{:S(2)}) %all-to-all-start.2) | async-done | bytes 49184 | tf_op jit(solution)/shard_map/all_to_all | solution.py:68
  53.7 0.1 reshape.90
  53.8 108.2 %all-gather.3.cloned.1.call-done = bf16[8192,384]{1,0:T(8,128)(2,1)} async-done(((bf16[128,384]{1,0:T(8,128)(2,1)}), bf16[8192,384]{1,0:T(8,128)(2,1)}) %all-gather.3.cloned.1.call-update) | async-done | bytes 6291472 | tf_op jit(solution)/shard_map/all_gather | solution.py:18
  162.0 6.6 %fusion.40 = (bf16[8192,192]{1,0:T(8,128)(2,1)}, bf16[8192,192]{1,0:T(8,128)(2,1)}) fusion(bf16[8192,384]{1,0:T(8,128)(2,1)} %all-gather.3.cloned.1.call-done), kind=kLoop, calls=%fused_computation.54 | loop fusion | bytes 12582912 | tf_op jit(solution)/shard_map/split | solution.py:19
  168.6 6.0 %copy.26 = bf16[8192,192]{0,1:T(8,128)(2,1)} copy(bf16[8192,192]{1,0:T(8,128)(2,1)} %get-tuple-element.6) | data formatting | bytes 6291456 | tf_op jit(solution)/shard_map/split | solution.py:19
  174.6 5.9 %copy.23 = bf16[8192,192]{0,1:T(8,128)(2,1)} copy(bf16[8192,192]{1,0:T(8,128)(2,1)} %get-tuple-element.5) | data formatting | bytes 6291456 | tf_op jit(solution)/shard_map/split | solution.py:19
  180.5 4.2 bitcast_reduce_fusion
  184.7 1.6 fusion.1
  186.3 0.2 copy-done.1
  186.6 0.0 copy-start.5
  186.6 2.5 fusion.25
  189.1 1.0 convolution_convert_fusion.1
  190.1 8.6 %all-to-all-start.3 = ((bf16[8,16,1536]{2,1,0:T(8,128)(2,1)}), bf16[8,16,1536]{2,1,0:T(8,128)(2,1)S(1)}, u32[]{:S(2)}, u32[]{:S(2)}) async-start(bf16[8,16,1536]{2,1,0:T(8,128)(2,1)} %bitcast.11), calls=%async_computation.3 | async-start | bytes 786432 | tf_op jit(solution)/shard_map/all_to_all | solution.py:29
  198.7 0.0 all-gather.5.cloned.1.call-start
  198.8 0.1 fusion.33
  198.8 0.1 reduce_window_sum.11
  198.9 0.2 select_reduce_fusion
  199.1 10.6 %all-to-all-done.3 = bf16[8,16,1536]{2,1,0:T(8,128)(2,1)S(1)} async-done(((bf16[8,16,1536]{2,1,0:T(8,128)(2,1)}), bf16[8,16,1536]{2,1,0:T(8,128)(2,1)S(1)}, u32[]{:S(2)}, u32[]{:S(2)}) %all-to-all-start.3) | async-done | bytes 393248 | tf_op jit(solution)/shard_map/all_to_all | solution.py:29
  209.7 0.1 convert_reduce_fusion
  209.8 0.1 fusion.39
  209.9 0.2 multiply_reduce_fusion.1
  210.1 0.0 copy-done.5
  210.1 0.1 add_convert_fusion.1
  210.2 0.1 broadcast_in_dim.8
  210.3 0.9 scatter_custom_fusion
  211.2 0.1 all_to_all.71
  211.4 25.9 %all_to_all.84 = bf16[64,2,1536]{2,1,0:T(2,128)(2,1)S(1)} all-to-all(bf16[64,2,1536]{2,1,0:T(2,128)(2,1)S(1)} %all_to_all.71), channel_id=1, replica_groups=mesh['head_0'=2,'head_1'=4,'blk'=64] {'blk'}, dimensions={0} | all-to-all | bytes 786432 | tf_op jit(solution)/shard_map/all_to_all | solution.py:124
  237.3 0.9 all_to_all.73
  238.2 0.0 all-gather.5.cloned.1.call-update
  238.2 0.2 reduce-scatter.3.cloned.1.call-start
  238.4 79.7 %all-gather.5.cloned.1.call-done = bf16[1024,1536]{1,0:T(8,128)(2,1)} async-done(((bf16[128,1536]{1,0:T(8,128)(2,1)}), bf16[1024,1536]{1,0:T(8,128)(2,1)}) %all-gather.5.cloned.1.call-update) | async-done | bytes 3145744 | tf_op jit(solution)/shard_map/all_gather | solution.py:127
  318.1 7.8 %convolution_convert_fusion = bf16[1024,1536]{1,0:T(8,128)(2,1)} fusion(bf16[1,512,1536]{2,1,0:T(8,128)(2,1)S(1)} %copy-done, bf16[1024,1536]{1,0:T(8,128)(2,1)} %all-gather.5.cloned.1.call-done, bf16[1,1536,512]{2,1,0:T(8,128)(2,1)} %param.22), kind=kOutput, calls=%fused_computation.10 | convolution fusion | flops 3227516928 | bytes 9437184 | tf_op jit(solution)/shard_map/dot_general | solution.py:134
  325.9 3.8 copy.30
  329.7 0.0 reduce-scatter.3.cloned.1.call-update
  329.7 0.0 reduce-scatter.5.cloned.1.call-start
  329.7 48.2 %reduce-scatter.3.cloned.1.call-done = bf16[2,128,1536]{2,1,0:T(8,128)(2,1)} async-done(((bf16[8,128,1536]{2,1,0:T(8,128)(2,1)}), bf16[2,128,1536]{2,1,0:T(8,128)(2,1)}) %reduce-scatter.3.cloned.1.call-update) | async-done | bytes 786448 | tf_op jit(solution)/shard_map/reduce_scatter | solution.py:39
  378.0 0.0 reduce-scatter.5.cloned.1.call-update
  378.0 35.7 %reduce-scatter.5.cloned.1.call-done = bf16[1,128,1536]{2,1,0:T(8,128)(2,1)} async-done(((bf16[2,128,1536]{2,1,0:T(8,128)(2,1)}), bf16[1,128,1536]{2,1,0:T(8,128)(2,1)}) %reduce-scatter.5.cloned.1.call-update) | async-done | bytes 393232 | tf_op jit(solution)/shard_map/reduce_scatter | solution.py:39
  413.7 1.9 all_to_all.74
  415.6 13.3 %all-to-all-start.5 = ((bf16[64,2,1536]{2,1,0:T(2,128)(2,1)}), bf16[64,2,1536]{2,1,0:T(2,128)(2,1)S(1)}, u32[]{:S(2)}, u32[]{:S(2)}) async-start(bf16[64,2,1536]{2,1,0:T(2,128)(2,1)} %all_to_all.74), calls=%async_computation.7 | async-start | bytes 786432 | tf_op jit(solution)/shard_map/all_to_all | solution.py:139
  428.8 0.1 copy.31
  428.9 14.1 %all-to-all-done.5 = bf16[64,2,1536]{2,1,0:T(2,128)(2,1)S(1)} async-done(((bf16[64,2,1536]{2,1,0:T(2,128)(2,1)}), bf16[64,2,1536]{2,1,0:T(2,128)(2,1)S(1)}, u32[]{:S(2)}, u32[]{:S(2)}) %all-to-all-start.5) | async-done | bytes 393248 | tf_op jit(solution)/shard_map/all_to_all | solution.py:139
  443.0 0.1 all_to_all.76
  443.2 0.6 gather_fusion
  443.8 0.1 reshape.95
  443.9 0.3 multiply_reduce_fusion
  444.3 0.6 add_convert_fusion
  (23 shorter events, 0.1 us)
Async XLA Ops:
  6.5 311.6 %copy-start = (bf16[1,512,1536]{2,1,0:T(8,128)(2,1)S(1)}, bf16[1,512,1536]{2,1,0:T(8,128)(2,1)}, u32[]{:S(2)}) copy-start(bf16[1,512,1536]{2,1,0:T(8,128)(2,1)} %param.23) | copy-start | bytes 4718596
  8.2 19.3 %all-to-all-start.1 = ((bf16[16,8,192]{2,0,1:T(8,128)(2,1)}), bf16[16,8,192]{2,0,1:T(8,128)(2,1)S(1)}, u32[]{:S(2)}, u32[]{:S(2)}) async-start(bf16[16,8,192]{2,0,1:T(8,128)(2,1)} %copy.22), calls=%async_computation.1 | async-start | bytes 131072 | tf_op jit(solution)/shard_map/all_to_all | solution.py:70
  18.3 143.7 %all-gather.3.cloned.1.call-start = ((), (), s32[]{:S(2)}) async-start(), calls=%async_computation.8 | async-start | bytes 6389760 | tf_op jit(solution)/shard_map/all_gather | solution.py:18
  41.3 12.4 %all-to-all-start.2 = ((bf16[16,8,192]{2,0,1:T(8,128)(2,1)}), bf16[16,8,192]{2,0,1:T(8,128)(2,1)S(1)}, u32[]{:S(2)}, u32[]{:S(2)}) async-start(bf16[16,8,192]{2,0,1:T(8,128)(2,1)} %copy.24), calls=%async_computation.2 | async-start | bytes 131072 | tf_op jit(solution)/shard_map/all_to_all | solution.py:68
  184.7 1.9 copy-start.1
  186.6 2.5 copy-start.3
  186.6 12.5 %copy-start.7 = (f32[1536]{0:T(1024)S(1)}, f32[1536]{0:T(1024)}, u32[]{:S(2)}) copy-start(f32[1536]{0:T(1024)} %param.20) | copy-start | bytes 18436
  186.6 23.2 %copy-start.2 = (bf16[16,1536]{1,0:T(8,128)(2,1)S(1)}, bf16[16,1536]{1,0:T(8,128)(2,1)}, u32[]{:S(2)}) copy-start(bf16[16,1536]{1,0:T(8,128)(2,1)} %param.16) | copy-start | bytes 147460
  186.6 23.2 %copy-start.4 = (f32[1536]{0:T(1024)S(1)}, f32[1536]{0:T(1024)}, u32[]{:S(2)}) copy-start(f32[1536]{0:T(1024)} %param.18) | copy-start | bytes 18436
  186.6 23.5 %copy-start.5 = (f32[1536]{0:T(1024)S(1)}, f32[1536]{0:T(1024)}, u32[]{:S(2)}) copy-start(f32[1536]{0:T(1024)} %param.19) | copy-start | bytes 18436
  190.1 19.6 %all-to-all-start.3 = ((bf16[8,16,1536]{2,1,0:T(8,128)(2,1)}), bf16[8,16,1536]{2,1,0:T(8,128)(2,1)S(1)}, u32[]{:S(2)}, u32[]{:S(2)}) async-start(bf16[8,16,1536]{2,1,0:T(8,128)(2,1)} %bitcast.11), calls=%async_computation.3 | async-start | bytes 786432 | tf_op jit(solution)/shard_map/all_to_all | solution.py:29
  198.7 119.4 %all-gather.5.cloned.1.call-start = ((), (), s32[]{:S(2)}) async-start(), calls=%async_computation.9 | async-start | bytes 3538944 | tf_op jit(solution)/shard_map/all_gather | solution.py:127
  238.2 139.8 %reduce-scatter.3.cloned.1.call-start = ((), (), s32[]{:S(2)}) async-start(), calls=%async_computation.10 | async-start | bytes 3932160 | tf_op jit(solution)/shard_map/reduce_scatter | solution.py:39
  329.7 99.2 %copy-start.8 = (f32[16,2]{0,1:T(2,128)S(1)}, f32[16,2]{0,1:T(2,128)}, u32[]{:S(2)}) copy-start(f32[16,2]{0,1:T(2,128)} %param.25) | copy-start | bytes 388
  329.7 114.6 %copy-start.6 = (f32[1536]{0:T(1024)S(1)}, f32[1536]{0:T(1024)}, u32[]{:S(2)}) copy-start(f32[1536]{0:T(1024)} %param.21) | copy-start | bytes 18436
  329.7 84.0 %reduce-scatter.5.cloned.1.call-start = ((), (), s32[]{:S(2)}) async-start(), calls=%async_computation.11 | async-start | bytes 1179648 | tf_op jit(solution)/shard_map/reduce_scatter | solution.py:39
  415.6 27.4 %all-to-all-start.5 = ((bf16[64,2,1536]{2,1,0:T(2,128)(2,1)}), bf16[64,2,1536]{2,1,0:T(2,128)(2,1)S(1)}, u32[]{:S(2)}, u32[]{:S(2)}) async-start(bf16[64,2,1536]{2,1,0:T(2,128)(2,1)} %all_to_all.74), calls=%async_computation.7 | async-start | bytes 786432 | tf_op jit(solution)/shard_map/all_to_all | solution.py:139
Sparse Core Ops, SparseCore 0:
  39.8 122.0 all-gather.2
  238.3 79.7 all-gather.4
  329.8 48.0 reduce-scatter.2
  380.6 33.0 reduce-scatter.4
where the time goes:
time: 452 us; the launch traced here: 451 us
  waiting for transfers between devices  312 us (69%)
  blocking collectives  37.4 us (8%)
  starting transfers between devices  35.6 us (8%)
  local copies, waits for them, and re-layouts  32.7 us (7%)
  matrix products  15.5 us (3%)
  between operations  13.4 us (3%)
  other arithmetic  4.81 us (1%)
    all_gather x1, waiting for transfers between devices, sent_together(): result = lax.all_gather(both, axis, axis=dim, tiled=True)  108 us
    reduce_scatter x2, waiting for transfers between devices, reduced_to_own(): blocks = lax.psum_scatter(blocks, axes[k], scatter_dimension=0, tiled=True)  83.9 us
    all_gather x1, waiting for transfers between devices, on_device(): lax.all_gather(arrived, HEAD, axis=0, tiled=True)  79.7 us
    all_to_all x1, blocking collectives, on_device(): lax.all_to_all(send_buffer, 'blk', split_axis=0, concat_axis=0, tiled=True)  25.9 us
    split x3, local copies, waits for them, and re-layouts, sent_together(): jnp.split(result, [sum(widths[:k]) for k in range(1, len(widths))], axis=...  18.5 us
    all_to_all x1, waiting for transfers between devices, on_device(): lax.all_to_all(partial_sum.astype(jnp.bfloat16), 'blk', split_axis=0, con...  14.1 us
    all_to_all x1, starting transfers between devices, on_device(): lax.all_to_all(partial_sum.astype(jnp.bfloat16), 'blk', split_axis=0, con...  13.3 us
    all_to_all x1, blocking collectives, on_device(): lax.all_to_all(key_rows, HEAD, split_axis=1, concat_axis=0, tiled=True)  11.5 us
  transfers between devices with their start and end apart: 8, of which 8 were waited for; matrix products, arithmetic and copies ran while one was open for 1% of the time, Pallas kernels for 0%

commit v1 on v0

v1 whole, which is shorter than its diff:
```python
import math

import jax
import jax.numpy as jnp
from jax import lax
from jax.sharding import Mesh
from jax.sharding import PartitionSpec as P

HD = 64
TOPK = 2
SLOTS = 2
AXES = ("yh", "x", "yl", "z", "c")
HEAD = ("yh", "x")
BLK = ("yl", "z", "c")


def exchange(array, axis):
    return lax.all_to_all(array, axis, 0, 0, tiled=True)


def gathered(array, axis):
    copies = jnp.broadcast_to(array[None], (lax.axis_size(axis), *array.shape))
    return exchange(copies, axis)


def partner(array, axis):
    return lax.ppermute(array, axis, [(0, 1), (1, 0)])


def both_sides(array, axis):
    other = partner(array, axis)
    first = lax.axis_index(axis) == 0
    return jnp.stack([jnp.where(first, array, other), jnp.where(first, other, array)])


def in_pieces(values, count):
    pieces = []
    for _ in range(count):
        piece = lax.reduce_precision(values, 8, 7)
        pieces.append(piece)
        values = values - piece
    return pieces


def on_device(
    query_rows,
    key_rows,
    value_rows,
    residual,
    out_weight,
    attention_gate,
    norm_shift,
    norm_scale,
    expert_gate,
    expert_up,
    expert_down,
    routing,
    combine_weight,
):
    bf16, f32 = jnp.bfloat16, jnp.float32
    tok, width = query_rows.shape
    n_head = lax.axis_size(HEAD)
    n_x = lax.axis_size("x")
    n_z = lax.axis_size("z")
    experts = lax.axis_size(BLK)
    cols = width // n_head
    heads = cols // HD
    rows = n_head * tok

    residual_both = both_sides(residual, "yh").reshape(2 * tok, width)
    routed = jnp.concatenate([routing.astype(f32), combine_weight], axis=1)
    routed_both = both_sides(routed, "yh")
    choice = routed_both[:, :, :TOPK].astype(jnp.int32)
    weight = routed_both[:, :, TOPK:].reshape(2 * tok, TOPK)

    own = jnp.concatenate(
        [a.reshape(tok, n_head, cols) for a in (query_rows, key_rows, value_rows)], axis=2
    )
    own = exchange(jnp.transpose(own, (1, 0, 2)), HEAD).reshape(rows, 3 * cols)
    keys_values = gathered(own[:, cols:], "yl").reshape(-1, 2 * cols)
    keys_values = jnp.concatenate([keys_values, partner(keys_values, "c")], axis=0)
    queries = gathered(own[:, :cols], "z").reshape(-1, cols)

    q = queries.reshape(-1, heads, HD)
    k = keys_values[:, :cols].reshape(-1, heads, HD)
    v = keys_values[:, cols:].reshape(-1, heads, HD)
    scores = jnp.einsum("rhd,phd->hrp", q, k, preferred_element_type=f32) * (1.0 / math.sqrt(HD))
    peak = jnp.max(scores, axis=2)
    probs = jnp.exp(scores - peak[:, :, None])
    total = jnp.sum(probs, axis=2)
    accum = jnp.einsum("hrp,phd->hrd", probs.astype(bf16), v, preferred_element_type=f32)
    part = (accum / total[:, :, None]).astype(bf16)
    part = jnp.transpose(part, (1, 0, 2)).reshape(-1, cols)
    stats = jnp.concatenate(in_pieces(peak, 3) + in_pieces(total, 3), axis=0).astype(bf16).T
    stats = jnp.pad(stats, ((0, 0), (0, 64 - stats.shape[1])))
    packed = jnp.concatenate([part, stats], axis=1).reshape(n_z, rows, cols + 64)
    packed = exchange(packed, "z")
    parts = packed[:, :, :cols].astype(f32).reshape(n_z, rows, heads, HD)
    stats = packed[:, :, cols : cols + 6 * heads].astype(f32).reshape(n_z, rows, 6, heads)
    peaks = jnp.sum(stats[:, :, :3], axis=2)
    totals = jnp.sum(stats[:, :, 3:], axis=2)
    share = totals * jnp.exp(peaks - jnp.max(peaks, axis=0, keepdims=True))
    share = share / jnp.sum(share, axis=0, keepdims=True)
    attended = jnp.sum(parts * share[:, :, :, None], axis=0).reshape(rows, cols).astype(bf16)

    partial = jnp.dot(attended, out_weight, preferred_element_type=f32).astype(bf16)
    partial = partial.reshape(2, n_x, tok, width).transpose(1, 0, 2, 3).reshape(n_x, 2 * tok, width)
    summed = jnp.sum(exchange(partial, "x").astype(f32), axis=0)
    projected = summed + partner(summed.astype(bf16), "yh").astype(f32)

    middle = residual_both.astype(f32) + attention_gate * projected
    average = jnp.mean(middle, axis=1, keepdims=True)
    centered = middle - average
    variance = jnp.mean(centered * centered, axis=1, keepdims=True)
    normed = (centered * lax.rsqrt(variance + 1e-06) * (1.0 + norm_scale) + norm_shift).astype(bf16)

    flat = choice.reshape(2, -1)
    same = flat[:, :, None] == flat[:, None, :]
    order = jnp.arange(flat.shape[1])
    earlier = same & (order[None, None, :] < order[None, :, None])
    slot = jnp.sum(earlier.astype(jnp.int32), axis=2)
    source = jnp.arange(2, dtype=jnp.int32)[:, None]
    place = ((flat * 2 + source) * SLOTS + slot).reshape(2 * tok, TOPK)
    per_expert = 2 * SLOTS
    buffer_rows = experts * per_expert
    hit = place[:, :, None] == jnp.arange(buffer_rows, dtype=jnp.int32)[None, None, :]
    chosen = jnp.any(hit, axis=1).astype(bf16)
    sent = jnp.dot(chosen.T, normed, preferred_element_type=f32).astype(bf16)
    arrived = exchange(sent.reshape(experts, per_expert, width), BLK).reshape(buffer_rows, width)

    buffers = gathered(arrived, "x").reshape(n_x * buffer_rows, width)
    hidden = jax.nn.gelu(
        jnp.dot(buffers, expert_up[0], preferred_element_type=f32), approximate=True
    ).astype(bf16)
    output = jnp.dot(hidden, expert_down[0], preferred_element_type=f32).astype(bf16)
    output = exchange(output.reshape(n_x, buffer_rows, width), "x")
    output = jnp.sum(output.astype(f32), axis=0).astype(bf16)
    returned = exchange(output.reshape(experts, per_expert, width), BLK).reshape(buffer_rows, width)

    pick = jnp.sum(jnp.where(hit, weight[:, :, None], 0.0), axis=1)
    pick = jnp.concatenate(in_pieces(pick, 2), axis=0).astype(bf16)
    mixed = jnp.dot(pick, returned, preferred_element_type=f32).reshape(2, 2, tok, width)
    mixed = mixed[0] + mixed[1]
    side = lax.axis_index("yh") == 0
    kept = jnp.where(side, mixed[0], mixed[1])
    given = jnp.where(side, mixed[1], mixed[0]).astype(bf16)
    mixture = kept + partner(given, "yh").astype(f32)
    middle = middle.reshape(2, tok, width)
    middle = jnp.where(side, middle[0], middle[1])
    return (middle + expert_gate * mixture).astype(bf16)


def solution(mesh):
    split = Mesh(mesh.devices.reshape(2, 4, 4, 8, 2), AXES)
    everywhere = P(AXES, None)
    placed = (
        everywhere,
        everywhere,
        everywhere,
        everywhere,
        P(HEAD, None),
        P(),
        P(),
        P(),
        P(),
        P(BLK, None, HEAD),
        P(BLK, HEAD, None),
        everywhere,
        everywhere,
    )
    return jax.shard_map(
        on_device, mesh=split, in_specs=placed, out_specs=everywhere, check_vma=False
    )
```

time: 452 us -> 292 us (0.65)
  waiting for transfers between devices: 312 us -> 69.5 us
  blocking collectives: 37.4 us -> 131 us
  local copies, waits for them, and re-layouts: 32.7 us -> 12 us
  starting transfers between devices: 35.6 us -> 51.5 us
  between operations: 13.4 us -> 0.58 us
    all_gather x2 -> x0, waiting for transfers between devices: 188 us -> none  [the longest x1 108 us: sent_together(): result = lax.all_gather(both, axis, axis=dim, tiled=True)]
    all_to_all x2 -> x4, blocking collectives: 37.4 us -> 131 us  [exchange(): return lax.all_to_all(array, axis, 0, 0, tiled=True)]
    reduce_scatter x2 -> x0, waiting for transfers between devices: 83.9 us -> none  [reduced_to_own(): blocks = lax.psum_scatter(blocks, axes[k], scatter_dimension=0, tiled=True)]
    ppermute x0 -> x5, starting transfers between devices: none -> 19.9 us  [partner(): return lax.ppermute(array, axis, [(0, 1), (1, 0)])]
    split x3 -> x0, local copies, waits for them, and re-layouts: 18.5 us -> none  [sent_together(): jnp.split(result, [sum(widths[:k]) for k in range(1, len(widths))], axis=...]
    all_to_all x4 -> x5, waiting for transfers between devices: 40.2 us -> 56.8 us  [exchange(): return lax.all_to_all(array, axis, 0, 0, tiled=True)]
    ppermute x0 -> x5, waiting for transfers between devices: none -> 12.7 us  [partner(): return lax.ppermute(array, axis, [(0, 1), (1, 0)])]
    all_to_all x10 -> x2, local copies, waits for them, and re-layouts: 7.21 us -> 0.48 us  [exchange(): return lax.all_to_all(array, axis, 0, 0, tiled=True)]
  transfers between devices with their start and end apart: 8 -> 10, of which waited for: 8 -> 6; matrix products, arithmetic and copies ran while one was open for 1% -> 6% of each run, Pallas kernels for 0% -> 0%
where the time goes in v1:
time: 292 us; the launch traced here: 291 us
  blocking collectives  131 us (45%)
  waiting for transfers between devices  69.5 us (24%)
  starting transfers between devices  51.5 us (18%)
  matrix products  16.9 us (6%)
  local copies, waits for them, and re-layouts  12 us (4%)
  other arithmetic  8.86 us (3%)
    all_to_all x4, blocking collectives, exchange(): return lax.all_to_all(array, axis, 0, 0, tiled=True)  131 us
    all_to_all x5, waiting for transfers between devices, exchange(): return lax.all_to_all(array, axis, 0, 0, tiled=True)  56.8 us
    all_to_all x5, starting transfers between devices, exchange(): return lax.all_to_all(array, axis, 0, 0, tiled=True)  31.6 us
    ppermute x5, starting transfers between devices, partner(): return lax.ppermute(array, axis, [(0, 1), (1, 0)])  19.9 us
    ppermute x5, waiting for transfers between devices, partner(): return lax.ppermute(array, axis, [(0, 1), (1, 0)])  12.7 us
    dot_general x1, matrix products, on_device(): jnp.dot(hidden, expert_down[0], preferred_element_type=f32).astype(bf16)  7.3 us
    dot_general x1, matrix products, on_device(): jnp.einsum('hrp,phd->hrd', probs.astype(bf16), v, preferred_element_type=...  6.79 us
  transfers between devices with their start and end apart: 10, of which 6 were waited for; matrix products, arithmetic and copies ran while one was open for 6% of the time, Pallas kernels for 0%

profile of v1, /device:TPU:1, one launch (start us, length us, event | category | flops | bytes accessed | tf_op | source)
XLA Modules:
  0.0 290.6 jit_solution(604067974349031620)
XLA Ops:
  0.0 1.0 reshape.162
  1.1 0.9 reshape.163
  2.0 0.9 reshape.164
  3.0 0.1 maximum_bitcast_fusion
  3.1 19.5 %all_to_all.45 = bf16[8,16,576]{2,1,0:T(8,128)(2,1)S(1)} all-to-all(bf16[8,16,576]{2,1,0:T(8,128)(2,1)S(1)} %maximum_bitcast_fusion), channel_id=1, replica_groups=mesh['yh'=2,'x'=4,'yl'=4,'z'=8,'c'=2] {'yh','x'}, dimensions={0} | all-to-all | bytes 294912 | tf_op jit(solution)/shard_map/all_to_all | solution.py:18
  22.6 0.1 slice.72
  22.7 0.1 copy.98
  22.8 0.8 broadcast_in_dim.19
  23.6 3.5 %all-to-all-start.2 = ((bf16[4,128,384]{1,2,0:T(8,128)(2,1)}), bf16[4,128,384]{1,2,0:T(8,128)(2,1)S(1)}, u32[]{:S(2)}, u32[]{:S(2)}) async-start(bf16[4,128,384]{1,2,0:T(8,128)(2,1)} %broadcast_in_dim.19), calls=%async_computation.2 | async-start | bytes 786432 | tf_op jit(solution)/shard_map/all_to_all | solution.py:18
  27.1 0.1 copy.96
  27.2 9.3 %all-to-all-done.2 = bf16[4,128,384]{1,2,0:T(8,128)(2,1)S(1)} async-done(((bf16[4,128,384]{1,2,0:T(8,128)(2,1)}), bf16[4,128,384]{1,2,0:T(8,128)(2,1)S(1)}, u32[]{:S(2)}, u32[]{:S(2)}) %all-to-all-start.2) | async-done | bytes 393248 | tf_op jit(solution)/shard_map/all_to_all | solution.py:18
  36.5 0.8 broadcast_in_dim.18
  37.3 10.0 %all-to-all-start.1 = ((bf16[8,128,192]{1,2,0:T(8,128)(2,1)}), bf16[8,128,192]{1,2,0:T(8,128)(2,1)S(1)}, u32[]{:S(2)}, u32[]{:S(2)}) async-start(bf16[8,128,192]{1,2,0:T(8,128)(2,1)} %broadcast_in_dim.18), calls=%async_computation.1 | async-start | bytes 786432 | tf_op jit(solution)/shard_map/all_to_all | solution.py:18
  47.3 0.2 copy.99
  47.6 5.3 %collective-permute-start.1 = (bf16[512,384]{1,0:T(8,128)(2,1)S(1)}, bf16[512,384]{1,0:T(8,128)(2,1)}, u32[]{:S(2)}, u32[]{:S(2)}) collective-permute-start(bf16[512,384]{1,0:T(8,128)(2,1)S(1)} %bitcast.78), channel_id=1, source_target_pairs={{0,1},{1,0},{2,3},{3,2},{4,5},{5,4},{6,7},{7,6},{8,9},{9,8},{10,11... | collective-permute-start | bytes 1179656 | tf_op jit(solution)/shard_map/ppermute | solution.py:27
  52.9 2.2 collective-permute-start
  55.2 7.0 %collective-permute-start.3 = (f32[16,4]{0,1:T(4,128)S(1)}, f32[16,4]{0,1:T(4,128)S(1)}, u32[]{:S(2)}, u32[]{:S(2)}) collective-permute-start(f32[16,4]{0,1:T(4,128)S(1)} %pad_maximum_fusion.4), channel_id=1, source_target_pairs={{0,256},{256,0},{1,257},{257,1},{2,258},{258,2},{3,259},{259,3},{4... | collective-permute-start | bytes 776 | tf_op jit(solution)/shard_map/ppermute | solution.py:27
  62.2 0.3 copy.97
  62.5 0.2 reshape_reshape.3
  62.6 1.3 fusion.33
  63.9 0.2 copy.100
  64.1 1.9 multiply_reduce_fusion
  66.0 2.1 fusion.1
  68.1 2.5 copy-done.1
  70.6 0.3 concatenate.28
  70.9 0.2 copy.101
  71.1 6.8 %fusion.27 = bf16[1024,3,64]{0,2,1:T(8,128)(2,1)S(1)} fusion(bf16[1024,3,64]{0,2,1:T(8,128)(2,1)S(1)} %bitcast.76, f32[3,1024,1024]{1,2,0:T(8,128)} %copy-done.1, f32[3,1024]{1,0:T(4,128)S(1)} %get-tuple-element.25, f32[1024,3]{0,1:T(4,128)S(1)} %bitcast.85), kind=kOutput, calls=%fused_computation.26 | convolution fusion | flops 412483584 | bytes 13393920 | tf_op jit(solution)/shard_map/hrp,phd->hrd/dot_general | solution.py:91
  78.0 0.8 pad_maximum_fusion.1
  78.9 7.1 %all-to-all-start.3 = ((bf16[8,128,256]{1,2,0:T(8,128)(2,1)}), bf16[8,128,256]{1,2,0:T(8,128)(2,1)S(1)}, u32[]{:S(2)}, u32[]{:S(2)}) async-start(bf16[8,128,256]{1,2,0:T(8,128)(2,1)} %pad_maximum_fusion.1), calls=%async_computation.3 | async-start | bytes 1048576 | tf_op jit(solution)/shard_map/all_to_all | solution.py:18
  86.1 0.1 copy.110
  86.2 0.1 eq.34
  86.3 0.2 convert_reduce_fusion.1
  86.5 0.1 reduce_sum.111
  86.5 0.1 copy.111
  86.6 0.1 mul.107
  86.7 0.1 fusion.40
  86.8 17.1 %all-to-all-done.3 = bf16[8,128,256]{1,2,0:T(8,128)(2,1)S(1)} async-done(((bf16[8,128,256]{1,2,0:T(8,128)(2,1)}), bf16[8,128,256]{1,2,0:T(8,128)(2,1)S(1)}, u32[]{:S(2)}, u32[]{:S(2)}) %all-to-all-start.3) | async-done | bytes 524320 | tf_op jit(solution)/shard_map/all_to_all | solution.py:18
  103.9 0.1 fusion.62
  104.1 0.1 fusion.30
  104.2 0.3 convolution_convert_fusion.2
  104.5 0.8 copy.108
  105.2 3.5 %all-to-all-start.4 = ((bf16[4,32,1536]{2,1,0:T(8,128)(2,1)}), bf16[4,32,1536]{2,1,0:T(8,128)(2,1)S(1)}, u32[]{:S(2)}, u32[]{:S(2)}) async-start(bf16[4,32,1536]{2,1,0:T(8,128)(2,1)} %bitcast.16), calls=%async_computation.4 | async-start | bytes 786432 | tf_op jit(solution)/shard_map/all_to_all | solution.py:18
  108.7 7.6 %all-to-all-done.4 = bf16[4,32,1536]{2,1,0:T(8,128)(2,1)S(1)} async-done(((bf16[4,32,1536]{2,1,0:T(8,128)(2,1)}), bf16[4,32,1536]{2,1,0:T(8,128)(2,1)S(1)}, u32[]{:S(2)}, u32[]{:S(2)}) %all-to-all-start.4) | async-done | bytes 393248 | tf_op jit(solution)/shard_map/all_to_all | solution.py:18
  116.4 2.2 collective-permute-start.2
  118.6 7.2 %collective-permute-done.2 = bf16[32,1536]{1,0:T(8,128)(2,1)S(1)} collective-permute-done((bf16[32,1536]{1,0:T(8,128)(2,1)S(1)}, bf16[32,1536]{1,0:T(8,128)(2,1)S(1)}, u32[]{:S(2)}, u32[]{:S(2)}) %collective-permute-start.2) | collective-permute-done | bytes 98336 | tf_op jit(solution)/shard_map/ppermute | solution.py:27
  125.8 0.2 fusion.60
  126.0 0.2 multiply_reduce_fusion.1
  126.2 0.4 convolution_convert_fusion.1
  126.7 0.2 reshape.173
  126.9 28.9 %all_to_all.46 = bf16[64,4,1536]{2,1,0:T(4,128)(2,1)S(1)} all-to-all(bf16[64,4,1536]{2,1,0:T(4,128)(2,1)S(1)} %reshape.173), channel_id=1, replica_groups=mesh['yh'=2,'x'=4,'yl'=4,'z'=8,'c'=2] {'yl','z','c'}, dimensions={0} | all-to-all | bytes 1572864 | tf_op jit(solution)/shard_map/all_to_all | solution.py:18
  155.8 0.2 broadcast_in_dim.23
  156.0 0.2 broadcast_in_dim.24
  156.2 40.9 %all_to_all.47 = bf16[4,256,1536]{2,1,0:T(8,128)(2,1)} all-to-all(bf16[4,256,1536]{2,1,0:T(8,128)(2,1)S(1)} %broadcast_in_dim.24), channel_id=1, replica_groups=mesh['yh'=2,'x'=4,'yl'=4,'z'=8,'c'=2] {'x'}, dimensions={0} | all-to-all | bytes 6291456 | tf_op jit(solution)/shard_map/all_to_all | solution.py:18
  197.1 7.3 %convolution_convert_fusion = bf16[1024,1536]{1,0:T(8,128)(2,1)} fusion(bf16[1,512,1536]{2,1,0:T(8,128)(2,1)S(1)} %copy-done, bf16[1024,1536]{1,0:T(8,128)(2,1)} %bitcast.73, bf16[1,1536,512]{2,1,0:T(8,128)(2,1)S(1)} %copy-done.10), kind=kOutput, calls=%fused_computation.6 | convolution fusion | flops 3227516928 | bytes 9437184 | tf_op jit(solution)/shard_map/dot_general | solution.py:135
  204.4 41.9 %all_to_all.48 = bf16[4,256,1536]{2,1,0:T(8,128)(2,1)} all-to-all(bf16[4,256,1536]{2,1,0:T(8,128)(2,1)} %bitcast.74), channel_id=1, replica_groups=mesh['yh'=2,'x'=4,'yl'=4,'z'=8,'c'=2] {'x'}, dimensions={0} | all-to-all | bytes 6291456 | tf_op jit(solution)/shard_map/all_to_all | solution.py:18
  246.3 2.8 reduce_sum.115
  249.1 1.1 reshape.176
  250.1 7.6 %all-to-all-start.8 = ((bf16[64,4,1536]{2,1,0:T(4,128)(2,1)}), bf16[64,4,1536]{2,1,0:T(4,128)(2,1)S(1)}, u32[]{:S(2)}, u32[]{:S(2)}) async-start(bf16[64,4,1536]{2,1,0:T(4,128)(2,1)} %reshape.176), calls=%async_computation.8 | async-start | bytes 1572864 | tf_op jit(solution)/shard_map/all_to_all | solution.py:18
  257.9 22.8 %all-to-all-done.8 = bf16[64,4,1536]{2,1,0:T(4,128)(2,1)S(1)} async-done(((bf16[64,4,1536]{2,1,0:T(4,128)(2,1)}), bf16[64,4,1536]{2,1,0:T(4,128)(2,1)S(1)}, u32[]{:S(2)}, u32[]{:S(2)}) %all-to-all-start.8) | async-done | bytes 786464 | tf_op jit(solution)/shard_map/all_to_all | solution.py:18
  280.7 0.2 reshape.177
  280.9 0.2 fusion.44
  281.2 3.2 %collective-permute-start.4 = (bf16[16,1536]{1,0:T(8,128)(2,1)S(1)}, bf16[16,1536]{1,0:T(8,128)(2,1)S(1)}, u32[]{:S(2)}, u32[]{:S(2)}) collective-permute-start(bf16[16,1536]{1,0:T(8,128)(2,1)S(1)} %select_convert_fusion), channel_id=1, source_target_pairs={{0,256},{256,0},{1,257},{257,1},{2,258},{258,2},{3,259},{259,3},{4... | collective-permute-start | bytes 147464 | tf_op jit(solution)/shard_map/ppermute | solution.py:27
  284.4 5.5 %collective-permute-done.4 = bf16[16,1536]{1,0:T(8,128)(2,1)S(1)} collective-permute-done((bf16[16,1536]{1,0:T(8,128)(2,1)S(1)}, bf16[16,1536]{1,0:T(8,128)(2,1)S(1)}, u32[]{:S(2)}, u32[]{:S(2)}) %collective-permute-start.4) | collective-permute-done | bytes 49184 | tf_op jit(solution)/shard_map/ppermute | solution.py:27
  290.0 0.7 fusion.35
  (62 shorter events, 0.8 us)
Async XLA Ops:
  0.0 197.1 %copy-start = (bf16[1,512,1536]{2,1,0:T(8,128)(2,1)S(1)}, bf16[1,512,1536]{2,1,0:T(8,128)(2,1)}, u32[]{:S(2)}) copy-start(bf16[1,512,1536]{2,1,0:T(8,128)(2,1)} %param.23) | copy-start | bytes 4718596
  0.0 52.9 %copy-start.3 = (bf16[16,1536]{1,0:T(8,128)(2,1)S(1)}, bf16[16,1536]{1,0:T(8,128)(2,1)}, u32[]{:S(2)}) copy-start(bf16[16,1536]{1,0:T(8,128)(2,1)} %param.16) | copy-start | bytes 147460
  0.0 55.1 %copy-start.9 = (s32[16,2]{0,1:T(2,128)S(1)}, s32[16,2]{0,1:T(2,128)}, u32[]{:S(2)}) copy-start(s32[16,2]{0,1:T(2,128)} %param.24) | copy-start | bytes 388
  0.0 55.1 %copy-start.8 = (f32[16,2]{0,1:T(2,128)S(1)}, f32[16,2]{0,1:T(2,128)}, u32[]{:S(2)}) copy-start(f32[16,2]{0,1:T(2,128)} %param.25) | copy-start | bytes 388
  23.6 12.9 %all-to-all-start.2 = ((bf16[4,128,384]{1,2,0:T(8,128)(2,1)}), bf16[4,128,384]{1,2,0:T(8,128)(2,1)S(1)}, u32[]{:S(2)}, u32[]{:S(2)}) async-start(bf16[4,128,384]{1,2,0:T(8,128)(2,1)} %broadcast_in_dim.19), calls=%async_computation.2 | async-start | bytes 786432 | tf_op jit(solution)/shard_map/all_to_all | solution.py:18
  37.3 24.9 %all-to-all-start.1 = ((bf16[8,128,192]{1,2,0:T(8,128)(2,1)}), bf16[8,128,192]{1,2,0:T(8,128)(2,1)S(1)}, u32[]{:S(2)}, u32[]{:S(2)}) async-start(bf16[8,128,192]{1,2,0:T(8,128)(2,1)} %broadcast_in_dim.18), calls=%async_computation.1 | async-start | bytes 786432 | tf_op jit(solution)/shard_map/all_to_all | solution.py:18
  47.6 15.1 %collective-permute-start.1 = (bf16[512,384]{1,0:T(8,128)(2,1)S(1)}, bf16[512,384]{1,0:T(8,128)(2,1)}, u32[]{:S(2)}, u32[]{:S(2)}) collective-permute-start(bf16[512,384]{1,0:T(8,128)(2,1)S(1)} %bitcast.78), channel_id=1, source_target_pairs={{0,1},{1,0},{2,3},{3,2},{4,5},{5,4},{6,7},{7,6},{8,9},{9,8},{10,11... | collective-permute-start | bytes 1179656 | tf_op jit(solution)/shard_map/ppermute | solution.py:27
  52.9 55.8 %collective-permute-start = (bf16[16,1536]{1,0:T(8,128)(2,1)S(1)}, bf16[16,1536]{1,0:T(8,128)(2,1)S(1)}, u32[]{:S(2)}, u32[]{:S(2)}) collective-permute-start(bf16[16,1536]{1,0:T(8,128)(2,1)S(1)} %copy-done.3), channel_id=1, source_target_pairs={{0,256},{256,0},{1,257},{257,1},{2,258},{258,2},{3,259},{259,3},{4... | collective-permute-start | bytes 147464 | tf_op jit(solution)/shard_map/ppermute | solution.py:27
  55.2 30.9 %collective-permute-start.3 = (f32[16,4]{0,1:T(4,128)S(1)}, f32[16,4]{0,1:T(4,128)S(1)}, u32[]{:S(2)}, u32[]{:S(2)}) collective-permute-start(f32[16,4]{0,1:T(4,128)S(1)} %pad_maximum_fusion.4), channel_id=1, source_target_pairs={{0,256},{256,0},{1,257},{257,1},{2,258},{258,2},{3,259},{259,3},{4... | collective-permute-start | bytes 776 | tf_op jit(solution)/shard_map/ppermute | solution.py:27
  66.0 4.6 %copy-start.1 = (f32[3,1024,1024]{1,2,0:T(8,128)}, f32[3,1024,1024]{1,2,0:T(8,128)S(1)}, u32[]{:S(2)}) copy-start(f32[3,1024,1024]{1,2,0:T(8,128)S(1)} %get-tuple-element.26) | copy-start | bytes 37748740
  77.9 8.0 %copy-start.7 = (f32[1536]{0:T(1024)S(1)}, f32[1536]{0:T(1024)}, u32[]{:S(2)}) copy-start(f32[1536]{0:T(1024)} %param.20) | copy-start | bytes 18436
  77.9 26.3 %copy-start.2 = (bf16[192,1536]{1,0:T(8,128)(2,1)S(1)}, bf16[192,1536]{1,0:T(8,128)(2,1)}, u32[]{:S(2)}) copy-start(bf16[192,1536]{1,0:T(8,128)(2,1)} %param.17) | copy-start | bytes 1769476
  78.9 47.0 %copy-start.4 = (f32[1536]{0:T(1024)S(1)}, f32[1536]{0:T(1024)}, u32[]{:S(2)}) copy-start(f32[1536]{0:T(1024)} %param.18) | copy-start | bytes 18436
  78.9 25.0 %all-to-all-start.3 = ((bf16[8,128,256]{1,2,0:T(8,128)(2,1)}), bf16[8,128,256]{1,2,0:T(8,128)(2,1)S(1)}, u32[]{:S(2)}, u32[]{:S(2)}) async-start(bf16[8,128,256]{1,2,0:T(8,128)(2,1)} %pad_maximum_fusion.1), calls=%async_computation.3 | async-start | bytes 1048576 | tf_op jit(solution)/shard_map/all_to_all | solution.py:18
  85.9 40.3 %copy-start.5 = (f32[1536]{0:T(1024)S(1)}, f32[1536]{0:T(1024)}, u32[]{:S(2)}) copy-start(f32[1536]{0:T(1024)} %param.19) | copy-start | bytes 18436
  105.2 11.1 %all-to-all-start.4 = ((bf16[4,32,1536]{2,1,0:T(8,128)(2,1)}), bf16[4,32,1536]{2,1,0:T(8,128)(2,1)S(1)}, u32[]{:S(2)}, u32[]{:S(2)}) async-start(bf16[4,32,1536]{2,1,0:T(8,128)(2,1)} %bitcast.16), calls=%async_computation.4 | async-start | bytes 786432 | tf_op jit(solution)/shard_map/all_to_all | solution.py:18
  116.4 9.4 %collective-permute-start.2 = (bf16[32,1536]{1,0:T(8,128)(2,1)S(1)}, bf16[32,1536]{1,0:T(8,128)(2,1)S(1)}, u32[]{:S(2)}, u32[]{:S(2)}) collective-permute-start(bf16[32,1536]{1,0:T(8,128)(2,1)S(1)} %convert_element_type.79), channel_id=1, source_target_pairs={{0,256},{256,0},{1,257},{257,1},{2,258},{258,2},{3,259},{259,3},{4... | collective-permute-start | bytes 294920 | tf_op jit(solution)/shard_map/ppermute | solution.py:27
  156.2 40.9 %copy-start.10 = (bf16[1,1536,512]{2,1,0:T(8,128)(2,1)S(1)}, bf16[1,1536,512]{2,1,0:T(8,128)(2,1)}, u32[]{:S(2)}) copy-start(bf16[1,1536,512]{2,1,0:T(8,128)(2,1)} %param.22) | copy-start | bytes 4718596
  249.0 40.9 %copy-start.6 = (f32[1536]{0:T(1024)S(1)}, f32[1536]{0:T(1024)}, u32[]{:S(2)}) copy-start(f32[1536]{0:T(1024)} %param.21) | copy-start | bytes 18436
  250.1 30.6 %all-to-all-start.8 = ((bf16[64,4,1536]{2,1,0:T(4,128)(2,1)}), bf16[64,4,1536]{2,1,0:T(4,128)(2,1)S(1)}, u32[]{:S(2)}, u32[]{:S(2)}) async-start(bf16[64,4,1536]{2,1,0:T(4,128)(2,1)} %reshape.176), calls=%async_computation.8 | async-start | bytes 1572864 | tf_op jit(solution)/shard_map/all_to_all | solution.py:18
  281.2 8.8 %collective-permute-start.4 = (bf16[16,1536]{1,0:T(8,128)(2,1)S(1)}, bf16[16,1536]{1,0:T(8,128)(2,1)S(1)}, u32[]{:S(2)}, u32[]{:S(2)}) collective-permute-start(bf16[16,1536]{1,0:T(8,128)(2,1)S(1)} %select_convert_fusion), channel_id=1, source_target_pairs={{0,256},{256,0},{1,257},{257,1},{2,258},{258,2},{3,259},{259,3},{4... | collective-permute-start | bytes 147464 | tf_op jit(solution)/shard_map/ppermute | solution.py:27
